TPU v7x, 32 devices: a whole 2x2x4 slice. The times are simulated.
32 devices in a mesh: prow: 4 (over y, x), pcol: 8 (over z, core).
Axes of the slice: x: 2, y: 2, z: 4, core: 2. Of those that a mesh axis runs over, the one named last changes fastest.
Arguments:
- ancestor: float32 [12288, 12288], P('prow', 'pcol'), may hold values from -448 to 15360, as said below
- factor: bfloat16 [2, 12288, 256], P(None, 'prow'), may hold values from -0.0009765625 to 0.0009765625
- inverse_diag: bfloat16 [2, 256, 256], replicated, may hold values from -6 to 6
- block_mask: int32 [2, 48], replicated, may hold values 0 or 1
Outputs:
- column_block: float32 [2, 12288, 256], P(None, ('prow', 'pcol'))
- diagonal: float32 [2, 256, 256], replicated
Inputs may be any that keep to these rules, and one draw needn't show every extreme that they name: `ancestor`: symmetric.
All inputs are finite; a program needn't handle non-finite values.
Results may differ from a plain program's by a relative error of at most 0.0003.
Values may be sent and summed in bfloat16 or wider, within the bound.
A program may use at most 64 MiB of HBM per device.

v0:
```python
import jax
import jax.numpy as jnp
from jax import lax
from jax.sharding import PartitionSpec as P

WIDTH = 256


def split(x):
    high = lax.reduce_precision(x, 8, 7)
    low = x - high
    return (high.astype(jnp.bfloat16), low.astype(jnp.bfloat16))


def dot(a, b):
    return jnp.dot(a, b, preferred_element_type=jnp.float32)


def shards(ancestor, factor, inverse_diag, block_mask):
    rows_here = ancestor.shape[0]
    count, _, width = factor.shape
    n_rows = lax.axis_size("prow")
    n_cols = lax.axis_size("pcol")
    column = lax.axis_index("pcol")
    grid_row = lax.axis_index("prow")
    slab = rows_here // n_cols
    row_mask = jnp.repeat(block_mask, WIDTH, axis=1).astype(jnp.float32)
    own_mask = lax.dynamic_slice_in_dim(row_mask, grid_row * rows_here, rows_here, 1)
    masked = factor * own_mask[:, :, None].astype(factor.dtype)
    turned = masked.transpose(0, 2, 1).reshape(count * width, rows_here)
    high, low = split(ancestor)
    partial = dot(turned, high) + dot(turned, low)
    summed = lax.psum_scatter(partial, "prow", scatter_dimension=1, tiled=True)
    pairs = [(r * n_cols + c, c * n_rows + r) for r in range(n_rows) for c in range(n_cols)]
    placed = lax.ppermute(summed, ("prow", "pcol"), pairs)
    slab_mask = lax.dynamic_slice_in_dim(own_mask, column * slab, slab, 1)
    placed = placed.reshape(count, width, slab)
    column_block = -slab_mask[:, :, None] * placed.transpose(0, 2, 1)
    own_slab = lax.dynamic_slice_in_dim(masked, column * slab, slab, 1)
    high, low = split(column_block)
    term = jnp.stack(
        [dot(own_slab[k].T, high[k]) + dot(own_slab[k].T, low[k]) for k in range(count)]
    )
    total = lax.psum(term, ("prow", "pcol"))
    diagonal = inverse_diag.astype(jnp.float32) - total
    return (column_block, diagonal)


def solution(mesh):
    return jax.shard_map(
        shards,
        mesh=mesh,
        in_specs=(P("prow", "pcol"), P(None, "prow", None), P(), P()),
        out_specs=(P(None, ("prow", "pcol"), None), P()),
        check_vma=False,
    )
```

profile of v0, /device:TPU:0, one launch (start us, length us, event | category | flops | bytes accessed | tf_op | source)
XLA Modules:
  0.0 254.4 jit_solution(12898401769275026924)
XLA Ops:
  7.2 0.0 reduce-scatter.2.cloned.1.call-start
  7.2 0.7 convert_element_type.26
  7.9 0.1 broadcast_bitcast_fusion
  8.0 0.1 copy.9
  8.1 3.2 %copy.7 = bf16[2,3072,256]{1,2,0:T(8,128)(2,1)S(1)} copy(bf16[2,3072,256]{2,1,0:T(8,128)(2,1)} %param.5) | data formatting | bytes 6291456 | tf_op args[1]
  11.3 0.2 broadcast_multiply_fusion
  11.5 10.2 %fusion.1 = f32[512,1536]{1,0:T(8,128)S(1)} fusion(bf16[512,3072]{1,0:T(8,128)(2,1)S(1)} %bitcast.36, f32[3072,1536]{1,0:T(8,128)} %param.4), kind=kOutput, calls=%fused_computation.3 | convolution fusion | flops 4845993984 | bytes 25165824 | tf_op jit(solution)/shard_map/dot_general | solution.py:16
  21.7 11.2 %fusion.4 = f32[512,1536]{1,0:T(8,128)} fusion(f32[512,1536]{1,0:T(8,128)S(1)} %fusion.1, bf16[512,3072]{1,0:T(8,128)(2,1)S(1)} %bitcast.37, f32[3072,1536]{1,0:T(8,128)} %param.4), kind=kOutput, calls=%fused_computation.5 | convolution fusion | flops 4842061824 | bytes 28311552 | tf_op jit(solution)/shard_map/dot_general | solution.py:16
  33.0 0.0 reduce-scatter.2.cloned.1.call-update
  33.0 0.0 all-reduce.2.cloned.1.call-start
  33.0 46.7 %reduce-scatter.2.cloned.1.call-done = f32[512,384]{1,0:T(8,128)} async-done(((f32[512,1536]{1,0:T(8,128)}), f32[512,384]{1,0:T(8,128)}) %reduce-scatter.2.cloned.1.call-update) | async-done | bytes 786448 | tf_op jit(solution)/shard_map/reduce_scatter | solution.py:33
  79.8 1.8 collective-permute-start
  81.6 0.1 dynamic-slice_negate_fusion
  81.6 0.3 copy.8
  81.9 0.2 fusion.7
  82.1 0.0 copy-start.1
  82.2 1.4 fusion.9
  83.6 1.2 fusion.8
  84.8 1.2 fusion.5
  85.9 1.2 fusion.6
  87.1 0.8 pad_maximum_fusion
  87.9 0.0 all-reduce.2.cloned.1.call-update
  87.9 157.7 %all-reduce.2.cloned.1.call-done = f32[2,256,256]{2,1,0:T(8,128)} async-done(((f32[2,256,256]{2,1,0:T(8,128)}), f32[2,256,256]{2,1,0:T(8,128)}) %all-reduce.2.cloned.1.call-update) | async-done | bytes 524304 | tf_op jit(solution)/shard_map/psum | solution.py:44
  245.7 1.9 convert_subtract_fusion
  (8 shorter events, 0.1 us)
Async XLA Ops:
  7.2 72.6 %reduce-scatter.2.cloned.1.call-start = ((), (), s32[]{:S(2)}) async-start(), calls=%async_computation.1 | async-start | bytes 3932160 | tf_op jit(solution)/shard_map/reduce_scatter | solution.py:33
  11.5 10.2 %copy-start = (bf16[2,3072,256]{1,2,0:T(8,128)(2,1)}, bf16[2,3072,256]{1,2,0:T(8,128)(2,1)S(1)}, u32[]{:S(2)}) copy-start(bf16[2,3072,256]{1,2,0:T(8,128)(2,1)S(1)} %broadcast_multiply_fusion) | copy-start | bytes 9437188
  33.0 212.7 %all-reduce.2.cloned.1.call-start = ((), (), s32[]{:S(2)}) async-start(), calls=%async_computation.2 | async-start | bytes 1048576 | tf_op jit(solution)/shard_map/psum | solution.py:44
  79.8 1.9 collective-permute-start
  82.1 165.5 %copy-start.1 = (f32[2,384,256]{2,1,0:T(8,128)}, f32[2,384,256]{2,1,0:T(8,128)S(1)}, u32[]{:S(2)}) copy-start(f32[2,384,256]{2,1,0:T(8,128)S(1)} %get-tuple-element.3) | copy-start | bytes 2359300
  82.1 163.6 %copy-start.2 = (bf16[2,256,256]{2,1,0:T(8,128)(2,1)S(1)}, bf16[2,256,256]{2,1,0:T(8,128)(2,1)}, u32[]{:S(2)}) copy-start(bf16[2,256,256]{2,1,0:T(8,128)(2,1)} %param.6) | copy-start | bytes 786436
Sparse Core Ops, SparseCore 0:
  33.1 46.6 reduce-scatter.1
  88.1 157.5 all-reduce.1
where the time goes:
time: 255 us; the launch traced here: 254 us
  waiting for transfers between devices  205 us (80%)
  matrix products  26.3 us (10%)
  between operations  14.2 us (6%)
  other arithmetic  3.91 us (2%)
  local copies, waits for them, and re-layouts  3.65 us (1%)
    psum x1, waiting for transfers between devices, shards(): total = lax.psum(term, ('prow', 'pcol'))  158 us
    reduce_scatter x1, waiting for transfers between devices, shards(): summed = lax.psum_scatter(partial, 'prow', scatter_dimension=1, tiled=True)  46.7 us
    dot_general x6, matrix products, dot(): return jnp.dot(a, b, preferred_element_type=jnp.float32)  26.3 us
  transfers between devices with their start and end apart: 3, of which 2 were waited for; matrix products, arithmetic and copies ran while one was open for 0% of the time, Pallas kernels for 0%

commit v1 on v0

--- a/solution.py
+++ b/solution.py
@@ -41,7 +41,7 @@
     term = jnp.stack(
         [dot(own_slab[k].T, high[k]) + dot(own_slab[k].T, low[k]) for k in range(count)]
     )
-    total = lax.psum(term, ("prow", "pcol"))
+    total = jnp.sum(lax.all_gather(term, ("prow", "pcol")), axis=0)
     diagonal = inverse_diag.astype(jnp.float32) - total
     return (column_block, diagonal)
 

time: 255 us -> 246 us (0.965)
  waiting for transfers between devices: 205 us -> 190 us
  other arithmetic: 3.91 us -> 9.8 us
    psum x1 -> x0, waiting for transfers between devices: 158 us -> none  [shards(): total = lax.psum(term, ('prow', 'pcol'))]
    all_gather x0 -> x1, waiting for transfers between devices: none -> 143 us  [shards(): total = jnp.sum(lax.all_gather(term, ('prow', 'pcol')), axis=0)]
    reduce_sum x0 -> x1, other arithmetic: none -> 6.93 us  [shards(): total = jnp.sum(lax.all_gather(term, ('prow', 'pcol')), axis=0)]
where the time goes in v1:
time: 246 us
  waiting for transfers between devices  190 us (77%)
  matrix products  26.3 us (11%)
  between operations  14.2 us (6%)
  other arithmetic  9.8 us (4%)
  local copies, waits for them, and re-layouts  3.64 us (1%)
    all_gather x1, waiting for transfers between devices, shards(): total = jnp.sum(lax.all_gather(term, ('prow', 'pcol')), axis=0)  143 us
    reduce_scatter x1, waiting for transfers between devices, shards(): summed = lax.psum_scatter(partial, 'prow', scatter_dimension=1, tiled=True)  46.7 us
    dot_general x6, matrix products, dot(): return jnp.dot(a, b, preferred_element_type=jnp.float32)  26.3 us
    reduce_sum x1, other arithmetic, shards(): total = jnp.sum(lax.all_gather(term, ('prow', 'pcol')), axis=0)  6.93 us
  transfers between devices with their start and end apart: 3, of which 2 were waited for; matrix products, arithmetic and copies ran while one was open for 0% of the time, Pallas kernels for 0%

profile of v1, /device:TPU:0, one launch (start us, length us, event | category | flops | bytes accessed | tf_op | source)
XLA Modules:
  0.0 245.6 jit_solution(9798565877010183141)
XLA Ops:
  7.2 0.0 reduce-scatter.2.cloned.1.call-start
  7.2 0.7 convert_element_type.26
  7.9 0.1 broadcast_bitcast_fusion
  8.0 0.1 copy.11
  8.1 3.2 %copy.9 = bf16[2,3072,256]{1,2,0:T(8,128)(2,1)S(1)} copy(bf16[2,3072,256]{2,1,0:T(8,128)(2,1)} %param.5) | data formatting | bytes 6291456 | tf_op args[1]
  11.3 0.2 broadcast_multiply_fusion
  11.5 10.2 %fusion.1 = f32[512,1536]{1,0:T(8,128)S(1)} fusion(bf16[512,3072]{1,0:T(8,128)(2,1)S(1)} %bitcast.38, f32[3072,1536]{1,0:T(8,128)} %param.4), kind=kOutput, calls=%fused_computation.3 | convolution fusion | flops 4845993984 | bytes 25165824 | tf_op jit(solution)/shard_map/dot_general | solution.py:16
  21.7 11.2 %fusion.4 = f32[512,1536]{1,0:T(8,128)} fusion(f32[512,1536]{1,0:T(8,128)S(1)} %fusion.1, bf16[512,3072]{1,0:T(8,128)(2,1)S(1)} %bitcast.39, f32[3072,1536]{1,0:T(8,128)} %param.4), kind=kOutput, calls=%fused_computation.5 | convolution fusion | flops 4842061824 | bytes 28311552 | tf_op jit(solution)/shard_map/dot_general | solution.py:16
  33.0 0.0 reduce-scatter.2.cloned.1.call-update
  33.0 0.0 all-gather.3.cloned.1.call-start
  33.0 46.7 %reduce-scatter.2.cloned.1.call-done = f32[512,384]{1,0:T(8,128)} async-done(((f32[512,1536]{1,0:T(8,128)}), f32[512,384]{1,0:T(8,128)}) %reduce-scatter.2.cloned.1.call-update) | async-done | bytes 786448 | tf_op jit(solution)/shard_map/reduce_scatter | solution.py:33
  79.8 1.8 collective-permute-start
  81.6 0.1 dynamic-slice_negate_fusion
  81.6 0.3 copy.10
  81.9 0.2 fusion.7
  82.1 1.4 fusion.9
  83.5 1.2 fusion.8
  84.7 1.2 fusion.5
  85.9 1.2 fusion.6
  87.0 0.8 pad_maximum_fusion
  87.9 0.0 all-gather.3.cloned.1.call-update
  87.9 143.0 %all-gather.3.cloned.1.call-done = f32[64,256,256]{2,1,0:T(8,128)} async-done(((f32[2,256,256]{2,1,0:T(8,128)}), f32[64,256,256]{2,1,0:T(8,128)}) %all-gather.3.cloned.1.call-update) | async-done | bytes 16777232 | tf_op jit(solution)/shard_map/all_gather | solution.py:44
  230.9 6.9 %reduce_sum.9 = f32[2,256,256]{2,1,0:T(8,128)S(1)} reduce(f32[32,2,256,256]{3,2,1,0:T(8,128)} %bitcast.37, f32[]{:T(128)} %constant.28.clone.1), dimensions={0}, to_apply=%region_1.0 | reduce | flops 4063232 | bytes 17301508 | tf_op jit(solution)/shard_map/reduce_sum | solution.py:44
  237.9 0.8 convert_subtract_fusion
  (9 shorter events, 0.1 us)
Async XLA Ops:
  7.2 72.6 %reduce-scatter.2.cloned.1.call-start = ((), (), s32[]{:S(2)}) async-start(), calls=%async_computation.1 | async-start | bytes 3932160 | tf_op jit(solution)/shard_map/reduce_scatter | solution.py:33
  11.5 10.2 %copy-start = (bf16[2,3072,256]{1,2,0:T(8,128)(2,1)}, bf16[2,3072,256]{1,2,0:T(8,128)(2,1)S(1)}, u32[]{:S(2)}) copy-start(bf16[2,3072,256]{1,2,0:T(8,128)(2,1)S(1)} %broadcast_multiply_fusion) | copy-start | bytes 9437188
  33.0 197.9 %all-gather.3.cloned.1.call-start = ((), (), s32[]{:S(2)}) async-start(), calls=%async_computation.2 | async-start | bytes 17301504 | tf_op jit(solution)/shard_map/all_gather | solution.py:44
  79.8 1.9 collective-permute-start
  82.1 155.8 %copy-start.1 = (f32[2,384,256]{2,1,0:T(8,128)}, f32[2,384,256]{2,1,0:T(8,128)S(1)}, u32[]{:S(2)}) copy-start(f32[2,384,256]{2,1,0:T(8,128)S(1)} %get-tuple-element.3) | copy-start | bytes 2359300
  230.9 6.9 %copy-start.2 = (bf16[2,256,256]{2,1,0:T(8,128)(2,1)S(1)}, bf16[2,256,256]{2,1,0:T(8,128)(2,1)}, u32[]{:S(2)}) copy-start(bf16[2,256,256]{2,1,0:T(8,128)(2,1)} %param.6) | copy-start | bytes 786436
Sparse Core Ops, SparseCore 0:
  33.1 46.6 reduce-scatter.1
  88.0 142.8 all-gather.2
